TPU v7x, 256 devices: a whole 4x4x8 slice. The times are simulated.
256 devices in a mesh: dp: 64 (over x, z, core), tensor: 4 (over y).
Axes of the slice: x: 4, y: 4, z: 8, core: 2. Of those that a mesh axis runs over, the one named last changes fastest.
Arguments:
- gate_preactivation: bfloat16 [1024, 28672], P('dp', 'tensor'), may hold values from -6 to 6
- up_preactivation: bfloat16 [1024, 28672], P('dp', 'tensor'), may hold values from -6 to 6
- cotangent: bfloat16 [1024, 8192], P('dp'), may hold values from -0.1875 to 0.1875
- down_weight: bfloat16 [28672, 8192], P('tensor', 'dp'), may hold values from -0.03125 to 0.03125
- lowrank_factor_first: bfloat16 [28672, 64], P('tensor'), may hold values from -0.03125 to 0.03125
- lowrank_factor_second: bfloat16 [64, 8192], replicated, may hold values from -0.75 to 0.75
- sparse_block_values: bfloat16 [64, 4, 2, 128, 128], P('dp', 'tensor'), may hold values from -0.5 to 0.5
- slot_block_rows: int32 [64, 4, 2], P(None, 'tensor'), may hold values from 0 to 55, as said below
- slot_block_columns: int32 [64, 4, 2], P(None, 'tensor'), may hold values from 0 to 0
- owner_slot_counts: int32 [64, 4], P(None, 'tensor'), may hold values from 1 to 2, as said below
Outputs:
- mixed: bfloat16 [1024, 8192], P('tensor', 'dp')
- grad_a: float32 [28672, 64], P('tensor')
- grad_b: float32 [64, 8192], P(None, 'dp')
- grad_blocks: float32 [64, 4, 2, 128, 128], P('dp', 'tensor')
Inputs may be any that keep to these rules, and one draw needn't show every extreme that they name: `slot_block_rows`: the 2 slots of one owner name different blocks. `owner_slot_counts`: some owner has exactly 2 live slots.
All inputs are finite; a program needn't handle non-finite values.
Results may differ from a plain program's by a relative error of at most 0.0049.
Values may be sent and summed in bfloat16 or wider, within the bound.
No kernel may reach another device: no remote copies, remote signals or barrier semaphores. Data moves between devices by JAX's collectives and lax.ppermute only.
A program may use at most 128 MiB of HBM per device.

v0:
```python
import jax
import jax.numpy as jnp
from jax import lax
from jax.sharding import Mesh
from jax.sharding import PartitionSpec as P

DP = ("dp_0", "dp_1", "dp_2")


def split_up(array, dim, count):
    before, after = (array.shape[:dim], array.shape[dim + 1 :])
    return jnp.moveaxis(array.reshape(*before, count, -1, *after), dim, 0)


def sent_and_summed(array, axis, dim):
    blocks = split_up(array, dim, lax.axis_size(axis))
    arrived = lax.all_to_all(blocks, axis, split_axis=0, concat_axis=0, tiled=True)
    return arrived.sum(axis=0)


def sent_to_all(array, axis):
    count = lax.axis_size(axis)
    return lax.all_to_all(
        jnp.broadcast_to(array[None], (count, *array.shape)), axis, 0, 0, tiled=True
    )


def of_everyone(array, axis):
    return sent_to_all(array, axis).sum(axis=0)


def joined_along(blocks, dim):
    blocks = jnp.moveaxis(blocks, 0, dim)
    lengths = blocks.shape
    return blocks.reshape(*lengths[:dim], lengths[dim] * lengths[dim + 1], *lengths[dim + 2 :])


def collect(array, axis, dim):
    return joined_along(sent_to_all(array, axis), dim)


def all_blocks(array, axes, turns):
    blocks = array
    for k in turns:
        blocks = lax.all_gather(blocks, axes[k])
    done = turns[::-1]
    back = [done.index(k) for k in range(len(axes))]
    blocks = blocks.transpose(*back, *range(len(axes), blocks.ndim))
    return blocks.reshape(-1, *array.shape)


def gathered_by_axis(array, axes, turns, dim):
    return joined_along(all_blocks(array, axes, turns), dim)


def column_view(cotangent):
    return lax.all_to_all(cotangent, DP, split_axis=1, concat_axis=0, tiled=True)


def shards(
    gate_preactivation,
    up_preactivation,
    cotangent,
    down_weight,
    lowrank_factor_first,
    lowrank_factor_second,
    sparse_block_values,
    slot_block_rows,
    slot_block_columns,
    owner_slot_counts,
):
    data_parallel_index = lax.axis_index(DP)
    column_offset = down_weight.shape[1]
    side = sparse_block_values.shape[-1]
    slots = sparse_block_values.shape[2]
    per_col = column_offset // side
    hidden_activation = (
        jax.nn.silu(gate_preactivation.astype(jnp.float32)) * up_preactivation.astype(jnp.float32)
    ).astype(jnp.bfloat16)
    hidden_gathered = lax.all_gather(hidden_activation, DP, axis=0, tiled=True)
    tok_all = hidden_gathered.shape[0]
    rows_all = slot_block_rows[:, 0, :]
    cols_all = slot_block_columns[:, 0, :]
    live_all = (
        jnp.arange(slots, dtype=jnp.int32)[None, :] < owner_slot_counts[:, 0][:, None]
    ).astype(jnp.float32)
    own_rows = lax.dynamic_index_in_dim(rows_all, data_parallel_index, 0, keepdims=False)
    own_cols = lax.dynamic_index_in_dim(cols_all, data_parallel_index, 0, keepdims=False)
    own_live = lax.dynamic_index_in_dim(live_all, data_parallel_index, 0, keepdims=False)
    factor_b_window = lax.dynamic_slice_in_dim(
        lowrank_factor_second, data_parallel_index * column_offset, column_offset, 1
    ).astype(jnp.float32)
    col_pick = (own_cols[:, None] == jnp.arange(per_col, dtype=jnp.int32)[None, :]).astype(
        jnp.float32
    ) * own_live[:, None]
    blocks = sparse_block_values[0, 0]
    owned_hidden = jnp.stack(
        [
            lax.dynamic_slice_in_dim(hidden_gathered, own_rows[slot] * side, side, 1)
            for slot in range(slots)
        ],
        axis=1,
    )
    total = jnp.dot(hidden_gathered, down_weight, preferred_element_type=jnp.float32)
    lowrank_token_rows = jnp.dot(
        hidden_gathered, lowrank_factor_first, preferred_element_type=jnp.float32
    )
    total = total + jnp.dot(lowrank_token_rows, factor_b_window, precision=lax.Precision.HIGHEST)
    local = jnp.einsum("tkc,kcd->tkd", owned_hidden, blocks, preferred_element_type=jnp.float32)
    spread = jnp.einsum("tkd,kn->tnd", local, col_pick, precision=lax.Precision.HIGHEST)
    summed = sent_and_summed(
        total
        + spread.reshape(
            tok_all // lax.axis_size("tensor") * lax.axis_size("tensor"), column_offset
        ),
        "tensor",
        0,
    )
    mixed = summed.astype(jnp.bfloat16)
    cotangent_lowrank = lax.dot_general(
        cotangent,
        lowrank_factor_second,
        (((1,), (1,)), ((), ())),
        preferred_element_type=jnp.float32,
    ).astype(jnp.bfloat16)
    lowrank_local_part = jnp.dot(
        hidden_activation, lowrank_factor_first, preferred_element_type=jnp.float32
    )
    cot_cols = None
    cot_cols = column_view(cotangent)
    low_full = of_everyone(lowrank_local_part, "tensor")
    low_all = collect(low_full, DP, 0)
    grad_b = lax.dot_general(
        low_all,
        cot_cols.astype(jnp.float32),
        (((0,), (0,)), ((), ())),
        precision=lax.Precision.HIGHEST,
    )
    cot_all = gathered_by_axis(cotangent_lowrank, DP, (0, 1, 2), 0)
    grad_a = lax.dot_general(
        hidden_gathered, cot_all, (((0,), (0,)), ((), ())), preferred_element_type=jnp.float32
    )
    pick_own = (own_cols[:, None] == jnp.arange(per_col, dtype=jnp.int32)[None, :]).astype(
        jnp.bfloat16
    )
    picked_c = jnp.einsum(
        "tnd,kn->tkd",
        cot_cols.reshape(tok_all, per_col, side),
        pick_own,
        preferred_element_type=jnp.float32,
    ).astype(jnp.bfloat16)
    owned = jnp.einsum("tkc,tkd->kcd", owned_hidden, picked_c, preferred_element_type=jnp.float32)
    grad_blocks = (owned * own_live[:, None, None])[None, None]
    return (mixed, grad_a, grad_b, grad_blocks)


def solution(mesh):
    finer = Mesh(
        mesh.devices.reshape(4, 8, 2, mesh.shape["tensor"]), ("dp_0", "dp_1", "dp_2", "tensor")
    )
    in_specs = (
        P(DP, "tensor"),
        P(DP, "tensor"),
        P(DP, None),
        P("tensor", DP),
        P("tensor", None),
        P(),
        P(DP, "tensor", None, None, None),
        P(None, "tensor", None),
        P(None, "tensor", None),
        P(None, "tensor"),
    )
    out_specs = (P("tensor", DP), P("tensor", None), P(None, DP), P(DP, "tensor", None, None, None))
    return jax.shard_map(
        shards, mesh=finer, in_specs=in_specs, out_specs=out_specs, check_vma=False
    )
```

profile of v0, /device:TPU:1, one launch (start us, length us, event | category | flops | bytes accessed | tf_op | source)
XLA Modules:
  0.0 160.6 jit_solution(10013752832817767674)
XLA Ops:
  7.2 2.1 %fusion.12 = bf16[16,7168]{1,0:T(8,128)(2,1)} fusion(bf16[16,7168]{1,0:T(8,128)(2,1)} %param.11, bf16[16,7168]{1,0:T(8,128)(2,1)} %param.10), kind=kLoop, calls=%fused_computation.20 | loop fusion | flops 917504 | bytes 688128 | tf_op jit(solution)/shard_map/convert_element_type | solution.py:79
  9.3 1.6 %fusion.27 = f32[16,64]{1,0:T(8,128)S(1)} fusion(bf16[16,7168]{1,0:T(8,128)(2,1)} %fusion.12, bf16[7168,64]{0,1:T(8,128)(2,1)} %param.14), kind=kOutput, calls=%fused_computation.43 | convolution fusion | flops 14680064 | bytes 1150976 | tf_op jit(solution)/shard_map/dot_general | solution.py:126
  11.7 5.0 %all-to-all-start.1 = ((f32[4,1,1024]{2,1,0:T(1,128)}), f32[4,1,1024]{2,1,0:T(1,128)S(1)}, u32[]{:S(2)}, u32[]{:S(2)}) async-start(f32[4,1,1024]{2,1,0:T(1,128)} %reshape.70), calls=%async_computation.1 | async-start | bytes 32768 | tf_op jit(solution)/shard_map/all_to_all | solution.py:23
  16.7 1.7 %copy_bitcast_fusion = bf16[16,64,128]{2,0,1:T(8,128)(2,1)} fusion(bf16[16,8192]{1,0:T(8,128)(2,1)} %param.12), kind=kLoop, calls=%fused_computation.21 | loop fusion | bytes 524288 | tf_op jit(solution)/shard_map/all_to_all | solution.py:57
  18.4 2.5 %all-to-all-done.1 = f32[4,1,1024]{2,1,0:T(1,128)S(1)} async-done(((f32[4,1,1024]{2,1,0:T(1,128)}), f32[4,1,1024]{2,1,0:T(1,128)S(1)}, u32[]{:S(2)}, u32[]{:S(2)}) %all-to-all-start.1) | async-done | bytes 16416 | tf_op jit(solution)/shard_map/all_to_all | solution.py:23
  20.9 13.6 %all-to-all-start.3 = ((bf16[16,64,128]{2,0,1:T(8,128)(2,1)}), bf16[16,64,128]{2,0,1:T(8,128)(2,1)S(1)}, u32[]{:S(2)}, u32[]{:S(2)}) async-start(bf16[16,64,128]{2,0,1:T(8,128)(2,1)} %copy_bitcast_fusion), calls=%async_computation.3 | async-start | bytes 524288 | tf_op jit(solution)/shard_map/all_to_all | solution.py:57
  35.3 1.7 %convolution_convert_fusion = bf16[16,64]{1,0:T(8,128)(2,1)S(1)} fusion(bf16[16,8192]{1,0:T(8,128)(2,1)} %param.12, bf16[64,8192]{1,0:T(8,128)(2,1)} %param.15), kind=kOutput, calls=%fused_computation.6 | convolution fusion | flops 16778240 | bytes 1312768 | tf_op jit(solution)/shard_map/dot_general | solution.py:120
  39.4 9.2 %all-to-all-done.3 = bf16[16,64,128]{2,0,1:T(8,128)(2,1)S(1)} async-done(((bf16[16,64,128]{2,0,1:T(8,128)(2,1)}), bf16[16,64,128]{2,0,1:T(8,128)(2,1)S(1)}, u32[]{:S(2)}, u32[]{:S(2)}) %all-to-all-start.3) | async-done | bytes 262176 | tf_op jit(solution)/shard_map/all_to_all | solution.py:57
  48.6 6.4 %all-to-all-start.2 = ((f32[64,1,1024]{2,1,0:T(1,128)}), f32[64,1,1024]{2,1,0:T(1,128)}, u32[]{:S(2)}, u32[]{:S(2)}) async-start(f32[64,1,1024]{2,1,0:T(1,128)} %reshape.72), calls=%async_computation.2 | async-start | bytes 524288 | tf_op jit(solution)/shard_map/all_to_all | solution.py:23
  56.8 1.2 dynamic-slice.2
  58.9 10.5 %all-gather = bf16[64,64]{1,0:T(8,128)(2,1)S(1)} all-gather(bf16[16,64]{1,0:T(8,128)(2,1)S(1)} %convolution_convert_fusion), channel_id=2, replica_groups=mesh['dp_0'=4,'dp_1'=8,'dp_2'=2,'tensor'=4] {'dp_0'}, dimensions={0}, use_global_device_ids=true | all-gather | bytes 10240 | tf_op jit(solution)/shard_map/all_gather | solution.py:45
  69.4 22.0 %all-gather.1 = bf16[32,16,64]{2,1,0:T(8,128)(2,1)S(1)} all-gather(bf16[4,16,64]{2,1,0:T(8,128)(2,1)S(1)} %bitcast.65), channel_id=3, replica_groups=mesh['dp_0'=4,'dp_1'=8,'dp_2'=2,'tensor'=4] {'dp_1'}, dimensions={0}, use_global_device_ids=true | all-gather | bytes 73728 | tf_op jit(solution)/shard_map/all_gather | solution.py:45
  91.3 8.6 %all-gather.2 = bf16[16,4,16,64]{3,2,1,0:T(8,128)(2,1)S(1)} all-gather(bf16[8,4,16,64]{3,2,1,0:T(8,128)(2,1)S(1)} %bitcast.63), channel_id=4, replica_groups=mesh['dp_0'=4,'dp_1'=8,'dp_2'=2,'tensor'=4] {'dp_2'}, dimensions={0}, use_global_device_ids=true | all-gather | bytes 196608 | tf_op jit(solution)/shard_map/all_gather | solution.py:45
  101.6 2.2 %reduce.3 = f32[64,1024]{1,0:T(8,128)S(1)} reduce(f32[64,1,1024]{2,1,0:T(1,128)} %all-to-all-done.2, f32[]{:T(128)} %broadcast.31), dimensions={1}, to_apply=%all_to_all.23.reduce_sub_computation | reduce | bytes 524292 | tf_op jit(solution)/shard_map/all_to_all | solution.py:23
  104.7 2.2 %convolution_bitcast_fusion.1 = f32[64,128]{1,0:T(8,128)} fusion(f32[64,16,64]{2,1,0:T(8,128)} %reshape.73, bf16[16,64,128]{2,0,1:T(8,128)(2,1)S(1)} %all-to-all-done.3), kind=kOutput, calls=%fused_computation.5 | convolution fusion | flops 100663296 | bytes 557056 | tf_op jit(solution)/shard_map/dot_general | solution.py:133
  107.0 5.6 %all-gather.5.cloned.1.call-done = bf16[1024,7168]{1,0:T(8,128)(2,1)} async-done(((bf16[16,7168]{1,0:T(8,128)(2,1)}), bf16[1024,7168]{1,0:T(8,128)(2,1)}) %all-gather.5.cloned.1.call-update) | async-done | bytes 14680080 | tf_op jit(solution)/shard_map/all_gather | solution.py:80
  112.6 1.2 dynamic-slice_bitcast_fusion.1
  113.8 1.3 convolution_bitcast_fusion
  115.2 7.9 %fusion.2 = f32[1,1024,128]{2,0,1:T(1,128)S(1)} fusion(f32[1024,2,128]{2,0,1:T(8,128)S(1)} %convolution_bitcast_fusion, pred[2]{0:T(512)(128)(4,1)S(1)} %compare_reduce_fusion, s32[1]{0:T(128)} %dynamic-slice.2), kind=kOutput, calls=%fused_computation.8 | convolution fusion | flops 3145734 | bytes 1572870 | tf_op jit(solution)/shard_map/tkd,kn->tnd/dot_general | solution.py:110
  123.1 9.7 %fusion.25 = f32[1024,64]{0,1:T(8,128)S(1)} fusion(bf16[1024,7168]{1,0:T(8,128)(2,1)} %all-gather.5.cloned.1.call-done, bf16[7168,64]{0,1:T(8,128)(2,1)S(1)} %copy-done.2), kind=kOutput, calls=%fused_computation.41 | convolution fusion | flops 939524096 | bytes 15859712 | tf_op jit(solution)/shard_map/dot_general | solution.py:105
  132.8 4.0 %fusion.24 = f32[1024,128]{1,0:T(8,128)S(1)} fusion(bf16[1024,7168]{1,0:T(8,128)(2,1)S(1)} %copy-done.1, bf16[7168,128]{1,0:T(8,128)(2,1)S(1)} %copy-done), kind=kOutput, calls=%fused_computation.40 | convolution fusion | flops 1879048192 | bytes 17039360 | tf_op jit(solution)/shard_map/dot_general | solution.py:104
  136.8 2.2 %fusion = f32[1024,128]{1,0:T(8,128)} fusion(f32[1024,128]{1,0:T(8,128)S(1)} %bitcast.64, f32[1024,128]{1,0:T(8,128)S(1)} %fusion.24, f32[1024,64]{0,1:T(8,128)S(1)} %fusion.25, bf16[64,8192]{1,0:T(8,128)(2,1)} %param.15, s32[]{:T(128)S(6)} %select_n.16), kind=kOutput, calls=%fused_computation.2 | convolution fusion | flops 100925440 | bytes 1851396 | tf_op jit(solution)/shard_map/dot_general | solution.py:108
  138.9 3.9 %all-to-all-start = ((f32[4,256,128]{2,1,0:T(8,128)}), f32[4,256,128]{2,1,0:T(8,128)S(1)}, u32[]{:S(2)}, u32[]{:S(2)}) async-start(f32[4,256,128]{2,1,0:T(8,128)} %bitcast.12), calls=%async_computation | async-start | bytes 1048576 | tf_op jit(solution)/shard_map/all_to_all | solution.py:17
  142.9 9.2 %fusion.26 = f32[7168,64]{0,1:T(8,128)} fusion(bf16[1024,7168]{1,0:T(8,128)(2,1)} %all-gather.5.cloned.1.call-done, bf16[1024,64]{1,0:T(8,128)(2,1)S(1)} %bitcast.61), kind=kOutput, calls=%fused_computation.42 | convolution fusion | flops 939524096 | bytes 16646144 | tf_op jit(solution)/shard_map/dot_general | solution.py:140
  (30 shorter events, 9.6 us)
Async XLA Ops:
  7.2 125.6 %copy-start = (bf16[7168,128]{1,0:T(8,128)(2,1)S(1)}, bf16[7168,128]{1,0:T(8,128)(2,1)}, u32[]{:S(2)}) copy-start(bf16[7168,128]{1,0:T(8,128)(2,1)} %param.13) | copy-start | bytes 5505028
  7.2 115.9 %copy-start.2 = (bf16[7168,64]{0,1:T(8,128)(2,1)S(1)}, bf16[7168,64]{0,1:T(8,128)(2,1)}, u32[]{:S(2)}) copy-start(bf16[7168,64]{0,1:T(8,128)(2,1)} %param.14) | copy-start | bytes 2752516
  7.2 105.4 %all-gather.5.cloned.1.call-start = ((), (), s32[]{:S(2)}) async-start(), calls=%async_computation.4 | async-start | bytes 14909440 | tf_op jit(solution)/shard_map/all_gather | solution.py:80
  11.7 9.2 %all-to-all-start.1 = ((f32[4,1,1024]{2,1,0:T(1,128)}), f32[4,1,1024]{2,1,0:T(1,128)S(1)}, u32[]{:S(2)}, u32[]{:S(2)}) async-start(f32[4,1,1024]{2,1,0:T(1,128)} %reshape.70), calls=%async_computation.1 | async-start | bytes 32768 | tf_op jit(solution)/shard_map/all_to_all | solution.py:23
  20.9 27.7 %all-to-all-start.3 = ((bf16[16,64,128]{2,0,1:T(8,128)(2,1)}), bf16[16,64,128]{2,0,1:T(8,128)(2,1)S(1)}, u32[]{:S(2)}, u32[]{:S(2)}) async-start(bf16[16,64,128]{2,0,1:T(8,128)(2,1)} %copy_bitcast_fusion), calls=%async_computation.3 | async-start | bytes 524288 | tf_op jit(solution)/shard_map/all_to_all | solution.py:57
  48.6 53.0 %all-to-all-start.2 = ((f32[64,1,1024]{2,1,0:T(1,128)}), f32[64,1,1024]{2,1,0:T(1,128)}, u32[]{:S(2)}, u32[]{:S(2)}) async-start(f32[64,1,1024]{2,1,0:T(1,128)} %reshape.72), calls=%async_computation.2 | async-start | bytes 524288 | tf_op jit(solution)/shard_map/all_to_all | solution.py:23
  112.6 20.2 %copy-start.1 = (bf16[1024,7168]{1,0:T(8,128)(2,1)S(1)}, bf16[1024,7168]{1,0:T(8,128)(2,1)}, u32[]{:S(2)}) copy-start(bf16[1024,7168]{1,0:T(8,128)(2,1)} %all-gather.5.cloned.1.call-done) | copy-start | bytes 44040196
  138.9 14.2 %all-to-all-start = ((f32[4,256,128]{2,1,0:T(8,128)}), f32[4,256,128]{2,1,0:T(8,128)S(1)}, u32[]{:S(2)}, u32[]{:S(2)}) async-start(f32[4,256,128]{2,1,0:T(8,128)} %bitcast.12), calls=%async_computation | async-start | bytes 1048576 | tf_op jit(solution)/shard_map/all_to_all | solution.py:17
  142.9 9.2 %copy-start.3 = (f32[1024,128]{1,0:T(8,128)S(1)}, f32[1024,128]{1,0:T(8,128)}, u32[]{:S(2)}) copy-start(f32[1024,128]{1,0:T(8,128)} %bitcast_convert_fusion) | copy-start | bytes 1572868
Sparse Core Ops, SparseCore 0:
  10.7 101.7 all-gather.4
where the time goes:
time: 161 us
  blocking collectives  41 us (25%)
  matrix products  40.9 us (25%)
  starting transfers between devices  29 us (18%)
  waiting for transfers between devices  17.4 us (11%)
  between operations  15.5 us (10%)
  local copies, waits for them, and re-layouts  8.89 us (6%)
  other arithmetic  8 us (5%)
    all_gather x3, blocking collectives, all_blocks(): blocks = lax.all_gather(blocks, axes[k])  41 us
    all_to_all x1, starting transfers between devices, column_view(): lax.all_to_all(cotangent, DP, split_axis=1, concat_axis=0, tiled=True)  13.6 us
    all_to_all x2, starting transfers between devices, sent_to_all(): lax.all_to_all(jnp.broadcast_to(array[None], (count, *array.shape)), axis...  11.4 us
    dot_general x1, matrix products, shards(): jnp.dot(hidden_gathered, lowrank_factor_first, preferred_element_type=jnp...  9.72 us
    all_to_all x1, waiting for transfers between devices, column_view(): lax.all_to_all(cotangent, DP, split_axis=1, concat_axis=0, tiled=True)  9.2 us
    dot_general x1, matrix products, shards(): lax.dot_general(hidden_gathered, cot_all, (((0,), (0,)), ((), ())), prefe...  9.19 us
    dot_general x1, matrix products, shards(): jnp.einsum('tkd,kn->tnd', local, col_pick, precision=lax.Precision.HIGHEST)  7.9 us
    all_gather x1, waiting for transfers between devices, shards(): hidden_gathered = lax.all_gather(hidden_activation, DP, axis=0, tiled=True)  5.64 us
  transfers between devices with their start and end apart: 5, of which 3 were waited for; matrix products, arithmetic and copies ran while one was open for 18% of the time, Pallas kernels for 0%

commit v1 on v0

--- a/solution.py
+++ b/solution.py
@@ -77,7 +77,9 @@
     hidden_activation = (
         jax.nn.silu(gate_preactivation.astype(jnp.float32)) * up_preactivation.astype(jnp.float32)
     ).astype(jnp.bfloat16)
-    hidden_gathered = lax.all_gather(hidden_activation, DP, axis=0, tiled=True)
+    hidden_gathered = jnp.concatenate(
+        lax.all_to_all(jnp.stack([hidden_activation] * lax.axis_size(DP)), DP, 0, 0), axis=0
+    )
     tok_all = hidden_gathered.shape[0]
     rows_all = slot_block_rows[:, 0, :]
     cols_all = slot_block_columns[:, 0, :]

time: 161 us -> 460 us (2.86)
  blocking collectives: 41 us -> 353 us
  between operations: 15.5 us -> 2.13 us
  local copies, waits for them, and re-layouts: 8.89 us -> 13.7 us
  waiting for transfers between devices: 17.4 us -> 12.7 us
    all_gather x3, blocking collectives: 41 us -> 335 us  [all_blocks(): blocks = lax.all_gather(blocks, axes[k])]
    all_to_all x0 -> x1, blocking collectives: none -> 17.9 us  [sent_to_all(): lax.all_to_all(jnp.broadcast_to(array[None], (count, *array.shape)), axis...]
    another operation x0 -> x1, local copies, waits for them, and re-layouts: none -> 7.01 us  [shards(): jnp.stack([hidden_activation] * lax.axis_size(DP))]
    all_to_all x2 -> x1, starting transfers between devices: 11.4 us -> 5 us  [sent_to_all(): lax.all_to_all(jnp.broadcast_to(array[None], (count, *array.shape)), axis...]
    all_to_all x0 -> x1, starting transfers between devices: none -> 6.34 us  [shards(): lax.all_to_all(jnp.stack([hidden_activation] * lax.axis_size(DP)), DP, 0, 0)]
    all_gather x1 -> x0, waiting for transfers between devices: 5.64 us -> none  [shards(): hidden_gathered = lax.all_gather(hidden_activation, DP, axis=0, tiled=True)]
  transfers between devices with their start and end apart: 5 -> 4, of which waited for: 3 -> 2; matrix products, arithmetic and copies ran while one was open for 18% -> 5% of each run, Pallas kernels for 0% -> 0%
where the time goes in v1:
time: 460 us
  blocking collectives  353 us (77%)
  matrix products  42.5 us (9%)
  starting transfers between devices  28.6 us (6%)
  local copies, waits for them, and re-layouts  13.7 us (3%)
  waiting for transfers between devices  12.7 us (3%)
  other arithmetic  6.66 us (1%)
    all_gather x3, blocking collectives, all_blocks(): blocks = lax.all_gather(blocks, axes[k])  335 us
    all_to_all x1, blocking collectives, sent_to_all(): lax.all_to_all(jnp.broadcast_to(array[None], (count, *array.shape)), axis...  17.9 us
    all_to_all x1, starting transfers between devices, column_view(): lax.all_to_all(cotangent, DP, split_axis=1, concat_axis=0, tiled=True)  13.6 us
    all_to_all x1, waiting for transfers between devices, column_view(): lax.all_to_all(cotangent, DP, split_axis=1, concat_axis=0, tiled=True)  10.2 us
    dot_general x1, matrix products, shards(): jnp.dot(hidden_gathered, lowrank_factor_first, preferred_element_type=jnp...  9.72 us
  transfers between devices with their start and end apart: 4, of which 2 were waited for; matrix products, arithmetic and copies ran while one was open for 5% of the time, Pallas kernels for 0%

profile of v1, /device:TPU:1, one launch (start us, length us, event | category | flops | bytes accessed | tf_op | source)
XLA Modules:
  0.0 459.5 jit_solution(17521848172262888403)
XLA Ops:
  0.6 1.3 fusion.12
  2.0 1.5 fusion.27
  4.2 5.0 %all-to-all-start.2 = ((f32[4,1,1024]{2,1,0:T(1,128)}), f32[4,1,1024]{2,1,0:T(1,128)S(1)}, u32[]{:S(2)}, u32[]{:S(2)}) async-start(f32[4,1,1024]{2,1,0:T(1,128)} %reshape.76), calls=%async_computation.2 | async-start | bytes 32768 | tf_op jit(solution)/shard_map/all_to_all | solution.py:23
  9.2 1.7 copy_bitcast_fusion
  10.9 2.5 all-to-all-done.2
  13.4 13.6 %all-to-all-start.4 = ((bf16[16,64,128]{2,0,1:T(8,128)(2,1)}), bf16[16,64,128]{2,0,1:T(8,128)(2,1)S(1)}, u32[]{:S(2)}, u32[]{:S(2)}) async-start(bf16[16,64,128]{2,0,1:T(8,128)(2,1)} %copy_bitcast_fusion), calls=%async_computation.4 | async-start | bytes 524288 | tf_op jit(solution)/shard_map/all_to_all | solution.py:57
  28.8 10.2 %all-to-all-done.4 = bf16[16,64,128]{2,0,1:T(8,128)(2,1)S(1)} async-done(((bf16[16,64,128]{2,0,1:T(8,128)(2,1)}), bf16[16,64,128]{2,0,1:T(8,128)(2,1)S(1)}, u32[]{:S(2)}, u32[]{:S(2)}) %all-to-all-start.4) | async-done | bytes 262176 | tf_op jit(solution)/shard_map/all_to_all | solution.py:57
  39.0 17.9 %all_to_all.36 = f32[64,1,1024]{2,1,0:T(1,128)} all-to-all(f32[64,1,1024]{2,1,0:T(1,128)S(1)} %reshape.78), channel_id=1, replica_groups=mesh['dp_0'=4,'dp_1'=8,'dp_2'=2,'tensor'=4] {'dp_0','dp_1','dp_2'}, dimensions={0} | all-to-all | bytes 524288 | tf_op jit(solution)/shard_map/all_to_all | solution.py:23
  56.9 7.0 %stack.8 = bf16[64,16,7168]{2,1,0:T(8,128)(2,1)} broadcast(bf16[16,7168]{1,0:T(8,128)(2,1)S(1)} %fusion.12), dimensions={1,2} | broadcast | bytes 14909440 | tf_op jit(solution)/shard_map/stack | solution.py:81
  63.9 6.3 %all-to-all-start = ((bf16[64,16,7168]{2,1,0:T(8,128)(2,1)}), bf16[64,16,7168]{2,1,0:T(8,128)(2,1)}, u32[]{:S(2)}, u32[]{:S(2)}) async-start(bf16[64,16,7168]{2,1,0:T(8,128)(2,1)} %stack.8), calls=%async_computation | async-start | bytes 29360128 | tf_op jit(solution)/shard_map/all_to_all | solution.py:81
  72.8 1.6 convolution_convert_fusion
  74.4 35.5 %all-gather = bf16[64,64]{1,0:T(8,128)(2,1)S(1)} all-gather(bf16[16,64]{1,0:T(8,128)(2,1)S(1)} %convolution_convert_fusion), channel_id=2, replica_groups=mesh['dp_0'=4,'dp_1'=8,'dp_2'=2,'tensor'=4] {'dp_0'}, dimensions={0}, use_global_device_ids=true | all-gather | bytes 10240 | tf_op jit(solution)/shard_map/all_gather | solution.py:45
  109.9 291.9 %all-gather.1 = bf16[32,16,64]{2,1,0:T(8,128)(2,1)S(1)} all-gather(bf16[4,16,64]{2,1,0:T(8,128)(2,1)S(1)} %bitcast.66), channel_id=3, replica_groups=mesh['dp_0'=4,'dp_1'=8,'dp_2'=2,'tensor'=4] {'dp_1'}, dimensions={0}, use_global_device_ids=true | all-gather | bytes 73728 | tf_op jit(solution)/shard_map/all_gather | solution.py:45
  401.7 8.0 %all-gather.2 = bf16[16,4,16,64]{3,2,1,0:T(8,128)(2,1)S(1)} all-gather(bf16[8,4,16,64]{3,2,1,0:T(8,128)(2,1)S(1)} %bitcast.64), channel_id=4, replica_groups=mesh['dp_0'=4,'dp_1'=8,'dp_2'=2,'tensor'=4] {'dp_2'}, dimensions={0}, use_global_device_ids=true | all-gather | bytes 196608 | tf_op jit(solution)/shard_map/all_gather | solution.py:45
  411.5 2.2 reduce.3
  414.7 2.3 convolution_bitcast_fusion.1
  417.0 9.7 %fusion.25 = f32[1024,64]{0,1:T(8,128)S(1)} fusion(bf16[1024,7168]{1,0:T(8,128)(2,1)} %bitcast, bf16[7168,64]{0,1:T(8,128)(2,1)S(1)} %copy-done.1), kind=kOutput, calls=%fused_computation.41 | convolution fusion | flops 939524096 | bytes 15859712 | tf_op jit(solution)/shard_map/dot_general | solution.py:107
  426.7 1.1 dynamic-slice_bitcast_fusion.1
  428.1 7.5 %fusion.2 = f32[1,1024,128]{2,0,1:T(1,128)S(1)} fusion(f32[1024,2,128]{2,0,1:T(8,128)S(1)} %convolution_bitcast_fusion, pred[2]{0:T(512)(128)(4,1)S(1)} %compare_reduce_fusion, s32[1]{0:T(128)} %dynamic-slice.2), kind=kOutput, calls=%fused_computation.8 | convolution fusion | flops 3145734 | bytes 1572870 | tf_op jit(solution)/shard_map/tkd,kn->tnd/dot_general | solution.py:112
  435.5 7.2 %fusion.24 = f32[1024,128]{1,0:T(8,128)S(1)} fusion(bf16[1024,7168]{1,0:T(8,128)(2,1)} %bitcast, bf16[7168,128]{1,0:T(8,128)(2,1)S(1)} %copy-done), kind=kOutput, calls=%fused_computation.40 | convolution fusion | flops 1879048192 | bytes 17039360 | tf_op jit(solution)/shard_map/dot_general | solution.py:106
  442.8 2.1 fusion
  444.9 3.7 all-to-all-start.1
  448.6 9.2 %fusion.26 = f32[7168,64]{0,1:T(8,128)} fusion(bf16[1024,7168]{1,0:T(8,128)(2,1)} %bitcast, bf16[1024,64]{1,0:T(8,128)(2,1)S(1)} %bitcast.62), kind=kOutput, calls=%fused_computation.42 | convolution fusion | flops 939524096 | bytes 16646144 | tf_op jit(solution)/shard_map/dot_general | solution.py:142
  457.8 1.0 fusion.1
  (37 shorter events, 7.3 us)
Async XLA Ops:
  0.6 434.9 %copy-start = (bf16[7168,128]{1,0:T(8,128)(2,1)S(1)}, bf16[7168,128]{1,0:T(8,128)(2,1)}, u32[]{:S(2)}) copy-start(bf16[7168,128]{1,0:T(8,128)(2,1)} %param.13) | copy-start | bytes 5505028
  4.2 9.2 %all-to-all-start.2 = ((f32[4,1,1024]{2,1,0:T(1,128)}), f32[4,1,1024]{2,1,0:T(1,128)S(1)}, u32[]{:S(2)}, u32[]{:S(2)}) async-start(f32[4,1,1024]{2,1,0:T(1,128)} %reshape.76), calls=%async_computation.2 | async-start | bytes 32768 | tf_op jit(solution)/shard_map/all_to_all | solution.py:23
  13.4 25.6 %all-to-all-start.4 = ((bf16[16,64,128]{2,0,1:T(8,128)(2,1)}), bf16[16,64,128]{2,0,1:T(8,128)(2,1)S(1)}, u32[]{:S(2)}, u32[]{:S(2)}) async-start(bf16[16,64,128]{2,0,1:T(8,128)(2,1)} %copy_bitcast_fusion), calls=%async_computation.4 | async-start | bytes 524288 | tf_op jit(solution)/shard_map/all_to_all | solution.py:57
  63.9 6.4 %copy-start.5 = (s32[64,1,2]{0,2,1:T(2,128)S(1)}, s32[64,1,2]{0,2,1:T(2,128)}, u32[]{:S(2)}) copy-start(s32[64,1,2]{0,2,1:T(2,128)} %param.17) | copy-start | bytes 1540
  63.9 8.3 %copy-start.7 = (s32[64,1]{0,1:T(1,128)S(1)}, s32[64,1]{0,1:T(1,128)}, u32[]{:S(2)}) copy-start(s32[64,1]{0,1:T(1,128)} %param.19) | copy-start | bytes 772
  63.9 8.9 %copy-start.2 = (bf16[16,8192]{1,0:T(8,128)(2,1)S(1)}, bf16[16,8192]{1,0:T(8,128)(2,1)}, u32[]{:S(2)}) copy-start(bf16[16,8192]{1,0:T(8,128)(2,1)} %param.12) | copy-start | bytes 786436
  63.9 345.9 %copy-start.6 = (s32[64,1,2]{0,2,1:T(2,128)S(1)}, s32[64,1,2]{0,2,1:T(2,128)}, u32[]{:S(2)}) copy-start(s32[64,1,2]{0,2,1:T(2,128)} %param.18) | copy-start | bytes 1540
  63.9 353.1 %copy-start.1 = (bf16[7168,64]{0,1:T(8,128)(2,1)S(1)}, bf16[7168,64]{0,1:T(8,128)(2,1)}, u32[]{:S(2)}) copy-start(bf16[7168,64]{0,1:T(8,128)(2,1)} %param.14) | copy-start | bytes 2752516
  63.9 353.1 %all-to-all-start = ((bf16[64,16,7168]{2,1,0:T(8,128)(2,1)}), bf16[64,16,7168]{2,1,0:T(8,128)(2,1)}, u32[]{:S(2)}, u32[]{:S(2)}) async-start(bf16[64,16,7168]{2,1,0:T(8,128)(2,1)} %stack.8), calls=%async_computation | async-start | bytes 29360128 | tf_op jit(solution)/shard_map/all_to_all | solution.py:81
  414.7 13.1 %copy-start.4 = (bf16[1,1,2,128,128]{4,3,2,1,0:T(8,128)(2,1)S(1)}, bf16[1,1,2,128,128]{4,3,2,1,0:T(8,128)(2,1)}, u32[]{:S(2)}) copy-start(bf16[1,1,2,128,128]{4,3,2,1,0:T(8,128)(2,1)} %param.16) | copy-start | bytes 196612
  444.9 13.9 %all-to-all-start.1 = ((f32[4,256,128]{2,1,0:T(8,128)}), f32[4,256,128]{2,1,0:T(8,128)S(1)}, u32[]{:S(2)}, u32[]{:S(2)}) async-start(f32[4,256,128]{2,1,0:T(8,128)} %bitcast.13), calls=%async_computation.1 | async-start | bytes 1048576 | tf_op jit(solution)/shard_map/all_to_all | solution.py:17
  448.6 9.2 %copy-start.3 = (f32[1024,128]{1,0:T(8,128)S(1)}, f32[1024,128]{1,0:T(8,128)}, u32[]{:S(2)}) copy-start(f32[1024,128]{1,0:T(8,128)} %bitcast_convert_fusion) | copy-start | bytes 1572868
